TPU v7x, 512 devices: a whole 4x4x16 slice. The times are simulated.
512 devices in a mesh: site: 32 (over x_hi, z), expert: 16 (over y, x_lo, core).
Axes of the slice: x: 4 (x_hi: 2, x_lo: 2; x = x_hi * 2 + x_lo), y: 4, z: 16, core: 2. Of those that a mesh axis runs over, the one named last changes fastest.
Arguments:
- out_grads: bfloat16 [2, 32, 2048, 1024], P(None, 'site', 'expert'), may hold values from -6 to 6
- routes: int32 [2, 32, 2048, 1], P(None, 'site', 'expert'), may hold values from 0 to 15; in each aligned block of 128 rows (0 to 127, 128 to 255, ..., all dimensions but the last counted through in order) at most 16 rows name the same one
- hiddens: bfloat16 [2, 32, 16, 256, 512], P(None, 'site', 'expert'), may hold values from -6 to 6
- weights: bfloat16 [32, 16, 512, 1024], P('site', 'expert'), may hold values from -6 to 6
- tracker_offset: bfloat16 [32, 16, 512, 1024], P('site', 'expert'), may hold values from -20 to 20
- partner_bits: int32 [32, 2], P('site'), may hold values from 0 to 1, as said below
Outputs:
- new_weights: bfloat16 [32, 16, 512, 1024], P('site', 'expert')
Inputs may be any that keep to these rules, and one draw needn't show every extreme that they name: `routes`: among the 128 tokens of one device in a step no expert is named more than 16 times, a bound that some block reaches. `partner_bits`: site 0 and site 32 - 1 each take the partner ahead in exactly one of the two rounds.
All inputs are finite; a program needn't handle non-finite values.
Results may differ from a plain program's by a relative error of at most 0.0095.
Values may be sent and summed in bfloat16 or wider, within the bound.
A program may use at most 64 MiB of HBM per device.

v0:
```python
import math

import jax
import jax.numpy as jnp
from jax import lax
from jax.sharding import PartitionSpec as P

NS_ITERS = 2


coef_a = 3.4445
coef_b = -4.775
coef_c = 2.0315
step_scale = 32.0
weight_hop = 4


def from_behind(block, axis, distance):
    devices = range(lax.axis_size(axis))
    route = [((i - distance) % len(devices), i) for i in devices]
    return lax.ppermute(block, axis, route)


def orthogonalize(tracked):
    frobenius = jnp.sqrt(jnp.sum(tracked * tracked))
    current = (tracked / (frobenius + 1e-07)).astype(jnp.bfloat16)
    for repeat in range(NS_ITERS):
        gram_matrix = lax.dot_general(
            current, current, (((1,), (1,)), ((), ())), preferred_element_type=jnp.float32
        ).astype(jnp.bfloat16)
        squared = jnp.dot(gram_matrix, gram_matrix, preferred_element_type=jnp.float32)
        polynomial = (coef_b * gram_matrix.astype(jnp.float32) + coef_c * squared).astype(
            jnp.bfloat16
        )
        current = (
            coef_a * current.astype(jnp.float32)
            + jnp.dot(polynomial, current, preferred_element_type=jnp.float32)
        ).astype(jnp.bfloat16)
    return current


def place_rows(gradient, routing, experts, slot_count):
    owned = (routing[:, None] == jnp.arange(experts, dtype=jnp.int32)[None, :]).astype(jnp.int32)
    earlier = jnp.cumsum(owned, axis=0) - owned
    position = jnp.sum(earlier * owned, axis=1)
    target = routing * slot_count + position
    selector = (
        target[None, :] == jnp.arange(experts * slot_count, dtype=jnp.int32)[:, None]
    ).astype(jnp.bfloat16)
    placed = jnp.dot(selector, gradient, preferred_element_type=jnp.float32).astype(jnp.bfloat16)
    return placed.reshape(experts, slot_count, gradient.shape[1])


def local_gradient(stashed, arrived):
    product = lax.dot_general(
        stashed, arrived, (((0,), (0,)), ((), ())), preferred_element_type=jnp.float32
    )
    return (product * (1.0 / math.sqrt(stashed.shape[0]))).astype(jnp.bfloat16)


def choose(ahead_value, behind, flag):
    return jnp.where(flag == 1, ahead_value, behind)


def local(out_grads, routes, hiddens, weights, tracker_offset, partner_bits):
    experts = lax.axis_size("expert")
    stashed = hiddens[:, 0, 0]
    step_count = stashed.shape[0]
    slot_rows = stashed.shape[1]
    slot_count = slot_rows // experts
    features = out_grads.shape[-1]
    direction = partner_bits[0]
    weight = weights[0, 0]
    offset = tracker_offset[0, 0]
    placed = [
        place_rows(out_grads[section_index, 0], routes[section_index, 0, :, 0], experts, slot_count)
        for section_index in range(step_count)
    ]
    arrived = [
        lax.all_to_all(outgoing, "expert", split_axis=0, concat_axis=0, tiled=True)
        for outgoing in placed
    ]
    gradients = [
        local_gradient(stashed[section_index], arrived[section_index].reshape(slot_rows, features))
        for section_index in range(step_count)
    ]
    own_updates = jnp.zeros(weight.shape, jnp.float32)
    for section_index in range(step_count):
        distance = 2**section_index
        gradient = gradients[section_index]
        summed = offset.astype(jnp.float32) + gradient.astype(jnp.float32)
        partner_sum = choose(
            from_behind(summed, "site", -distance),
            from_behind(summed, "site", distance),
            direction[section_index],
        )
        tracked = 0.5 * (summed + partner_sum)
        offset = (tracked - gradient.astype(jnp.float32)).astype(jnp.bfloat16)
        ortho = orthogonalize(tracked)
        own_updates = own_updates + ortho.astype(jnp.float32)
    updated = weight.astype(jnp.float32) - step_scale * own_updates
    beside_all = from_behind(updated.astype(jnp.bfloat16), "site", -weight_hop).astype(
        updated.dtype
    ) + from_behind(updated.astype(jnp.bfloat16), "site", weight_hop).astype(updated.dtype)
    result = (0.5 * updated + 0.25 * beside_all).astype(jnp.bfloat16)
    return result[None, None]


def solution(mesh):
    in_specs = (
        P(None, "site", "expert", None),
        P(None, "site", "expert", None),
        P(None, "site", "expert", None, None),
        P("site", "expert", None, None),
        P("site", "expert", None, None),
        P("site", None),
    )
    out_specs = P("site", "expert", None, None)
    return jax.shard_map(local, mesh=mesh, in_specs=in_specs, out_specs=out_specs, check_vma=False)
```

profile of v0, /device:TPU:104, one launch (start us, length us, event | category | flops | bytes accessed | tf_op | source)
XLA Modules:
  0.0 316.1 jit_solution(12220453429635055950)
XLA Ops:
  2.2 2.0 convolution_convert_fusion.5
  4.2 5.9 %all-to-all-start = ((bf16[16,16,1024]{2,1,0:T(8,128)(2,1)}), bf16[16,16,1024]{2,1,0:T(8,128)(2,1)S(1)}, u32[]{:S(2)}, u32[]{:S(2)}) async-start(bf16[16,16,1024]{2,1,0:T(8,128)(2,1)} %bitcast.4), calls=%async_computation | async-start | bytes 1048576 | tf_op jit(solution)/shard_map/all_to_all | solution.py:80
  10.6 7.7 %all-to-all-done = bf16[16,16,1024]{2,1,0:T(8,128)(2,1)S(1)} async-done(((bf16[16,16,1024]{2,1,0:T(8,128)(2,1)}), bf16[16,16,1024]{2,1,0:T(8,128)(2,1)S(1)}, u32[]{:S(2)}, u32[]{:S(2)}) %all-to-all-start) | async-done | bytes 524320 | tf_op jit(solution)/shard_map/all_to_all | solution.py:80
  18.3 1.8 convert_add_fusion
  20.1 2.0 collective-permute-start
  22.1 5.0 %collective-permute-start.1 = (f32[512,1024]{0,1:T(8,128)}, f32[512,1024]{0,1:T(8,128)}, u32[]{:S(2)}, u32[]{:S(2)}) collective-permute-start(f32[512,1024]{0,1:T(8,128)} %get-tuple-element.15), channel_id=1, source_target_pairs={{496,0},{0,16},{16,32},{32,48},{48,64},{64,80},{80,96},{96,112},{1... | collective-permute-start | bytes 6291464 | tf_op jit(solution)/shard_map/ppermute | solution.py:21
  28.3 6.1 %all-to-all-start.1 = ((bf16[16,16,1024]{2,1,0:T(8,128)(2,1)}), bf16[16,16,1024]{2,1,0:T(8,128)(2,1)S(1)}, u32[]{:S(2)}, u32[]{:S(2)}) async-start(bf16[16,16,1024]{2,1,0:T(8,128)(2,1)} %bitcast.11), calls=%async_computation.1 | async-start | bytes 1048576 | tf_op jit(solution)/shard_map/all_to_all | solution.py:80
  35.5 35.9 %collective-permute-done = f32[512,1024]{0,1:T(8,128)} collective-permute-done((f32[512,1024]{0,1:T(8,128)}, f32[512,1024]{0,1:T(8,128)}, u32[]{:S(2)}, u32[]{:S(2)}) %collective-permute-start) | collective-permute-done | bytes 2097184 | tf_op jit(solution)/shard_map/ppermute | solution.py:21
  72.6 4.3 %multiply_reduce_fusion.1 = (f32[]{:T(128)}, f32[512,1024]{0,1:T(8,128)}) fusion(f32[512,1024]{0,1:T(8,128)} %collective-permute-done, f32[512,1024]{0,1:T(8,128)} %collective-permute-done.1, pred[]{:T(512)} %bitcast.8, bf16[1024,512]{1,0:T(8,128)(2,1)S(1)} %get-tuple-element.16, bf16[1,1,512,1024]{2,3,1,0:T(8,128)(2,1)S(1)} %copy.8), kind=kLoop, calls=%fused_computation.15 | loop fusion | flops 4194303 | bytes 8388613 | tf_op jit(solution)/shard_map/reduce_sum | solution.py:25
  76.8 3.4 %bitcast_add_fusion = f32[512,1024]{0,1:T(8,128)} fusion(f32[512,1024]{0,1:T(8,128)} %get-tuple-element.6, bf16[1024,512]{1,0:T(8,128)(2,1)S(1)} %get-tuple-element.16, bf16[256,1024]{1,0:T(8,128)(2,1)S(1)} %bitcast.67, bf16[2,1,1,256,512]{4,3,2,1,0:T(8,128)(2,1)S(1)} %copy-done.2), kind=kOutput, calls=%fused_computation.2 | convolution fusion | flops 272629760 | bytes 6029312 | tf_op jit(solution)/shard_map/dot_general | solution.py:55
  80.2 10.8 %collective-permute-start.2 = (f32[512,1024]{0,1:T(8,128)}, f32[512,1024]{0,1:T(8,128)}, u32[]{:S(2)}, u32[]{:S(2)}) collective-permute-start(f32[512,1024]{0,1:T(8,128)} %bitcast_add_fusion), channel_id=1, source_target_pairs={{32,0},{48,16},{64,32},{80,48},{96,64},{112,80},{128,96},{144,112}... | collective-permute-start | bytes 6291464 | tf_op jit(solution)/shard_map/ppermute | solution.py:21
  91.0 1.9 collective-permute-start.3
  97.3 3.7 %add_convert_fusion.4 = bf16[512,1024]{0,1:T(8,128)(2,1)} fusion(bf16[512,512]{1,0:T(8,128)(2,1)} %convolution_convert_fusion.4, f32[512,1024]{0,1:T(8,128)S(1)} %copy-done, f32[]{:T(128)S(6)} %add.68), kind=kOutput, calls=%fused_computation.13 | convolution fusion | flops 810811392 | bytes 3670020 | tf_op jit(solution)/shard_map/dot_general | solution.py:37
  101.0 3.1 convolution_convert_fusion.3
  104.1 74.8 %collective-permute-done.2 = f32[512,1024]{0,1:T(8,128)} collective-permute-done((f32[512,1024]{0,1:T(8,128)}, f32[512,1024]{0,1:T(8,128)}, u32[]{:S(2)}, u32[]{:S(2)}) %collective-permute-start.2) | collective-permute-done | bytes 2097184 | tf_op jit(solution)/shard_map/ppermute | solution.py:21
  178.9 3.7 %multiply_reduce_fusion = (f32[]{:T(128)}, f32[512,1024]{0,1:T(8,128)S(1)}) fusion(f32[512,1024]{0,1:T(8,128)} %bitcast_add_fusion, f32[512,1024]{0,1:T(8,128)} %collective-permute-done.2, f32[512,1024]{0,1:T(8,128)} %collective-permute-done.3, pred[]{:T(512)} %bitcast.15), kind=kLoop, calls=%fused_computation.9 | loop fusion | flops 2621439 | bytes 8388613 | tf_op jit(solution)/shard_map/reduce_sum | solution.py:25
  184.8 3.5 %add_convert_fusion.2 = bf16[512,1024]{0,1:T(8,128)(2,1)} fusion(bf16[512,512]{1,0:T(8,128)(2,1)} %convolution_convert_fusion.1, f32[512,1024]{0,1:T(8,128)S(1)} %get-tuple-element.8, f32[]{:T(128)S(6)} %add.76), kind=kOutput, calls=%fused_computation.7 | convolution fusion | flops 810811392 | bytes 3670020 | tf_op jit(solution)/shard_map/dot_general | solution.py:37
  188.4 2.4 convolution_convert_fusion
  190.8 2.1 add_convert_fusion.1
  192.8 4.6 %fusion.47 = (bf16[512,1024]{0,1:T(8,128)(2,1)}, f32[512,1024]{0,1:T(8,128)S(1)}) fusion(bf16[512,1024]{0,1:T(8,128)(2,1)} %add_convert_fusion.1, bf16[512,1024]{0,1:T(8,128)(2,1)} %add_convert_fusion.4, bf16[512,512]{1,0:T(8,128)(2,1)} %convolution_convert_fusion.3, bf16[1,1,512,1024]{2,3,1,0:T(8,128)(2,1)S(1)} %copy.7), kind=kOutput, calls=%fused_computation.84 | convolution fusion | flops 812384256 | bytes 6815744 | tf_op jit(solution)/shard_map/dot_general | solution.py:37
  197.5 17.2 %collective-permute-start.4 = (bf16[512,1024]{0,1:T(8,128)(2,1)}, bf16[512,1024]{0,1:T(8,128)(2,1)S(1)}, u32[]{:S(2)}, u32[]{:S(2)}) collective-permute-start(bf16[512,1024]{0,1:T(8,128)(2,1)} %get-tuple-element.17), channel_id=1, source_target_pairs={{64,0},{80,16},{96,32},{112,48},{128,64},{144,80},{160,96},{176,11... | collective-permute-start | bytes 3145736 | tf_op jit(solution)/shard_map/ppermute | solution.py:21
  214.7 1.9 collective-permute-start.5
  216.6 69.3 %collective-permute-done.4 = bf16[512,1024]{0,1:T(8,128)(2,1)S(1)} collective-permute-done((bf16[512,1024]{0,1:T(8,128)(2,1)}, bf16[512,1024]{0,1:T(8,128)(2,1)S(1)}, u32[]{:S(2)}, u32[]{:S(2)}) %collective-permute-start.4) | collective-permute-done | bytes 1048608 | tf_op jit(solution)/shard_map/ppermute | solution.py:21
  285.9 28.4 %collective-permute-done.5 = bf16[512,1024]{0,1:T(8,128)(2,1)S(1)} collective-permute-done((bf16[512,1024]{0,1:T(8,128)(2,1)}, bf16[512,1024]{0,1:T(8,128)(2,1)S(1)}, u32[]{:S(2)}, u32[]{:S(2)}) %collective-permute-start.5) | collective-permute-done | bytes 1048608 | tf_op jit(solution)/shard_map/ppermute | solution.py:21
  (30 shorter events, 12.0 us)
Async XLA Ops:
  0.0 10.0 %copy-start.1 = (bf16[1,1,512,1024]{3,2,1,0:T(8,128)(2,1)S(1)}, bf16[1,1,512,1024]{3,2,1,0:T(8,128)(2,1)}, u32[]{:S(2)}) copy-start(bf16[1,1,512,1024]{3,2,1,0:T(8,128)(2,1)} %param.10) | copy-start | bytes 3145732
  1.1 17.2 %copy-start.2 = (bf16[2,1,1,256,512]{4,3,2,1,0:T(8,128)(2,1)S(1)}, bf16[2,1,1,256,512]{4,3,2,1,0:T(8,128)(2,1)}, u32[]{:S(2)}) copy-start(bf16[2,1,1,256,512]{4,3,2,1,0:T(8,128)(2,1)} %param.8) | copy-start | bytes 1572868
  4.2 14.1 %all-to-all-start = ((bf16[16,16,1024]{2,1,0:T(8,128)(2,1)}), bf16[16,16,1024]{2,1,0:T(8,128)(2,1)S(1)}, u32[]{:S(2)}, u32[]{:S(2)}) async-start(bf16[16,16,1024]{2,1,0:T(8,128)(2,1)} %bitcast.4), calls=%async_computation | async-start | bytes 1048576 | tf_op jit(solution)/shard_map/all_to_all | solution.py:80
  18.3 8.9 %copy-start.3 = (bf16[2,1,128,1024]{3,2,1,0:T(8,128)(2,1)S(1)}, bf16[2,1,128,1024]{3,2,1,0:T(8,128)(2,1)}, u32[]{:S(2)}) copy-start(bf16[2,1,128,1024]{3,2,1,0:T(8,128)(2,1)} %param.6) | copy-start | bytes 1572868
  18.3 16.1 %copy-start.4 = (s32[1,2]{1,0:T(1,128)S(1)}, s32[1,2]{1,0:T(1,128)}, u32[]{:S(2)}) copy-start(s32[1,2]{1,0:T(1,128)} %param.11) | copy-start | bytes 28
  20.1 51.2 %collective-permute-start = (f32[512,1024]{0,1:T(8,128)}, f32[512,1024]{0,1:T(8,128)}, u32[]{:S(2)}, u32[]{:S(2)}) collective-permute-start(f32[512,1024]{0,1:T(8,128)} %get-tuple-element.15), channel_id=1, source_target_pairs={{16,0},{32,16},{48,32},{64,48},{80,64},{96,80},{112,96},{128,112},... | collective-permute-start | bytes 6291464 | tf_op jit(solution)/shard_map/ppermute | solution.py:21
  22.1 50.4 %collective-permute-start.1 = (f32[512,1024]{0,1:T(8,128)}, f32[512,1024]{0,1:T(8,128)}, u32[]{:S(2)}, u32[]{:S(2)}) collective-permute-start(f32[512,1024]{0,1:T(8,128)} %get-tuple-element.15), channel_id=1, source_target_pairs={{496,0},{0,16},{16,32},{32,48},{48,64},{64,80},{80,96},{96,112},{1... | collective-permute-start | bytes 6291464 | tf_op jit(solution)/shard_map/ppermute | solution.py:21
  28.3 48.5 %all-to-all-start.1 = ((bf16[16,16,1024]{2,1,0:T(8,128)(2,1)}), bf16[16,16,1024]{2,1,0:T(8,128)(2,1)S(1)}, u32[]{:S(2)}, u32[]{:S(2)}) async-start(bf16[16,16,1024]{2,1,0:T(8,128)(2,1)} %bitcast.11), calls=%async_computation.1 | async-start | bytes 1048576 | tf_op jit(solution)/shard_map/all_to_all | solution.py:80
  80.2 15.6 %copy-start = (f32[512,1024]{0,1:T(8,128)S(1)}, f32[512,1024]{0,1:T(8,128)}, u32[]{:S(2)}) copy-start(f32[512,1024]{0,1:T(8,128)} %get-tuple-element.6) | copy-start | bytes 6291460
  80.2 98.6 %collective-permute-start.2 = (f32[512,1024]{0,1:T(8,128)}, f32[512,1024]{0,1:T(8,128)}, u32[]{:S(2)}, u32[]{:S(2)}) collective-permute-start(f32[512,1024]{0,1:T(8,128)} %bitcast_add_fusion), channel_id=1, source_target_pairs={{32,0},{48,16},{64,32},{80,48},{96,64},{112,80},{128,96},{144,112}... | collective-permute-start | bytes 6291464 | tf_op jit(solution)/shard_map/ppermute | solution.py:21
  91.0 87.9 %collective-permute-start.3 = (f32[512,1024]{0,1:T(8,128)}, f32[512,1024]{0,1:T(8,128)}, u32[]{:S(2)}, u32[]{:S(2)}) collective-permute-start(f32[512,1024]{0,1:T(8,128)} %bitcast_add_fusion), channel_id=1, source_target_pairs={{480,0},{496,16},{0,32},{16,48},{32,64},{48,80},{64,96},{80,112},{... | collective-permute-start | bytes 6291464 | tf_op jit(solution)/shard_map/ppermute | solution.py:21
  188.4 2.4 copy-start.5
  197.5 88.4 %collective-permute-start.4 = (bf16[512,1024]{0,1:T(8,128)(2,1)}, bf16[512,1024]{0,1:T(8,128)(2,1)S(1)}, u32[]{:S(2)}, u32[]{:S(2)}) collective-permute-start(bf16[512,1024]{0,1:T(8,128)(2,1)} %get-tuple-element.17), channel_id=1, source_target_pairs={{64,0},{80,16},{96,32},{112,48},{128,64},{144,80},{160,96},{176,11... | collective-permute-start | bytes 3145736 | tf_op jit(solution)/shard_map/ppermute | solution.py:21
  214.7 99.6 %collective-permute-start.5 = (bf16[512,1024]{0,1:T(8,128)(2,1)}, bf16[512,1024]{0,1:T(8,128)(2,1)S(1)}, u32[]{:S(2)}, u32[]{:S(2)}) collective-permute-start(bf16[512,1024]{0,1:T(8,128)(2,1)} %get-tuple-element.17), channel_id=1, source_target_pairs={{448,0},{464,16},{480,32},{496,48},{0,64},{16,80},{32,96},{48,112}... | collective-permute-start | bytes 3145736 | tf_op jit(solution)/shard_map/ppermute | solution.py:21
where the time goes:
time: 317 us; the launch traced here: 316 us
  waiting for transfers between devices  217 us (68%)
  starting transfers between devices  50.8 us (16%)
  matrix products  30.8 us (10%)
  other arithmetic  9.88 us (3%)
  local copies, waits for them, and re-layouts  4.75 us (1%)
    ppermute x6, waiting for transfers between devices, from_behind(): return lax.ppermute(block, axis, route)  209 us
    ppermute x6, starting transfers between devices, from_behind(): return lax.ppermute(block, axis, route)  38.8 us
    dot_general x4, matrix products, orthogonalize(): jnp.dot(polynomial, current, preferred_element_type=jnp.float32)  13.9 us
    all_to_all x2, starting transfers between devices, local(): lax.all_to_all(outgoing, 'expert', split_axis=0, concat_axis=0, tiled=True)  11.9 us
    dot_general x4, matrix products, orthogonalize(): lax.dot_general(current, current, (((1,), (1,)), ((), ())), preferred_ele...  8.55 us
    reduce_sum x2, other arithmetic, orthogonalize(): frobenius = jnp.sqrt(jnp.sum(tracked * tracked))  8.01 us
    all_to_all x2, waiting for transfers between devices, local(): lax.all_to_all(outgoing, 'expert', split_axis=0, concat_axis=0, tiled=True)  7.69 us
  transfers between devices with their start and end apart: 8, of which 6 were waited for; matrix products, arithmetic and copies ran while one was open for 5% of the time, Pallas kernels for 0%

commit v1 on v0

--- a/solution.py
+++ b/solution.py
@@ -89,11 +89,12 @@
         distance = 2**section_index
         gradient = gradients[section_index]
         summed = offset.astype(jnp.float32) + gradient.astype(jnp.float32)
+        sent = summed.astype(jnp.bfloat16)
         partner_sum = choose(
-            from_behind(summed, "site", -distance),
-            from_behind(summed, "site", distance),
+            from_behind(sent, "site", -distance),
+            from_behind(sent, "site", distance),
             direction[section_index],
-        )
+        ).astype(jnp.float32)
         tracked = 0.5 * (summed + partner_sum)
         offset = (tracked - gradient.astype(jnp.float32)).astype(jnp.bfloat16)
         ortho = orthogonalize(tracked)

time: 317 us -> 247 us (0.78)
  the two profiles are of different devices: /device:TPU:104 before, /device:TPU:41 now
where the time goes in v1:
time: 247 us; the launch traced here: 246 us
  waiting for transfers between devices  160 us (65%)
  starting transfers between devices  41.3 us (17%)
  matrix products  28 us (11%)
  other arithmetic  7.55 us (3%)
  local copies, waits for them, and re-layouts  6.55 us (3%)
  between operations  2.86 us (1%)
    ppermute x6, waiting for transfers between devices, from_behind(): return lax.ppermute(block, axis, route)  152 us
    ppermute x6, starting transfers between devices, from_behind(): return lax.ppermute(block, axis, route)  28.2 us
    all_to_all x2, starting transfers between devices, local(): lax.all_to_all(outgoing, 'expert', split_axis=0, concat_axis=0, tiled=True)  13.2 us
    dot_general x4, matrix products, orthogonalize(): jnp.dot(polynomial, current, preferred_element_type=jnp.float32)  13 us
    all_to_all x2, waiting for transfers between devices, local(): lax.all_to_all(outgoing, 'expert', split_axis=0, concat_axis=0, tiled=True)  7.69 us
    dot_general x4, matrix products, orthogonalize(): lax.dot_general(current, current, (((1,), (1,)), ((), ())), preferred_ele...  6.2 us
    dot_general x2, matrix products, local_gradient(): lax.dot_general(stashed, arrived, (((0,), (0,)), ((), ())), preferred_ele...  5.68 us
  transfers between devices with their start and end apart: 8, of which 7 were waited for; matrix products, arithmetic and copies ran while one was open for 6% of the time, Pallas kernels for 0%

profile of v1, /device:TPU:41, one launch (start us, length us, event | category | flops | bytes accessed | tf_op | source)
XLA Modules:
  0.0 246.0 jit_solution(5871178266693911218)
XLA Ops:
  2.2 2.0 convolution_convert_fusion.5
  4.2 6.1 %all-to-all-start = ((bf16[16,16,1024]{2,1,0:T(8,128)(2,1)}), bf16[16,16,1024]{2,1,0:T(8,128)(2,1)S(1)}, u32[]{:S(2)}, u32[]{:S(2)}) async-start(bf16[16,16,1024]{2,1,0:T(8,128)(2,1)} %bitcast.4), calls=%async_computation | async-start | bytes 1048576 | tf_op jit(solution)/shard_map/all_to_all | solution.py:80
  10.9 7.7 %all-to-all-done = bf16[16,16,1024]{2,1,0:T(8,128)(2,1)S(1)} async-done(((bf16[16,16,1024]{2,1,0:T(8,128)(2,1)}), bf16[16,16,1024]{2,1,0:T(8,128)(2,1)S(1)}, u32[]{:S(2)}, u32[]{:S(2)}) %all-to-all-start) | async-done | bytes 524320 | tf_op jit(solution)/shard_map/all_to_all | solution.py:80
  20.0 5.0 %collective-permute-start = (bf16[512,1024]{0,1:T(8,128)(2,1)}, bf16[512,1024]{0,1:T(8,128)(2,1)S(1)}, u32[]{:S(2)}, u32[]{:S(2)}) collective-permute-start(bf16[512,1024]{0,1:T(8,128)(2,1)} %get-tuple-element.14), channel_id=1, source_target_pairs={{16,0},{32,16},{48,32},{64,48},{80,64},{96,80},{112,96},{128,112},... | collective-permute-start | bytes 3145736 | tf_op jit(solution)/shard_map/ppermute | solution.py:21
  25.1 1.9 collective-permute-start.1
  28.1 7.0 %all-to-all-start.1 = ((bf16[16,16,1024]{2,1,0:T(8,128)(2,1)}), bf16[16,16,1024]{2,1,0:T(8,128)(2,1)}, u32[]{:S(2)}, u32[]{:S(2)}) async-start(bf16[16,16,1024]{2,1,0:T(8,128)(2,1)} %bitcast.11), calls=%async_computation.1 | async-start | bytes 1048576 | tf_op jit(solution)/shard_map/all_to_all | solution.py:80
  36.4 11.1 %collective-permute-done = bf16[512,1024]{0,1:T(8,128)(2,1)S(1)} collective-permute-done((bf16[512,1024]{0,1:T(8,128)(2,1)}, bf16[512,1024]{0,1:T(8,128)(2,1)S(1)}, u32[]{:S(2)}, u32[]{:S(2)}) %collective-permute-start) | collective-permute-done | bytes 1048608 | tf_op jit(solution)/shard_map/ppermute | solution.py:21
  47.5 10.7 %collective-permute-done.1 = bf16[512,1024]{0,1:T(8,128)(2,1)} collective-permute-done((bf16[512,1024]{0,1:T(8,128)(2,1)}, bf16[512,1024]{0,1:T(8,128)(2,1)}, u32[]{:S(2)}, u32[]{:S(2)}) %collective-permute-start.1) | collective-permute-done | bytes 1048608 | tf_op jit(solution)/shard_map/ppermute | solution.py:21
  60.2 4.2 %fusion.1 = (bf16[512,1024]{0,1:T(8,128)(2,1)}, bf16[512,1024]{0,1:T(8,128)(2,1)S(1)}, bf16[512,1024]{0,1:T(8,128)(2,1)}, bf16[1024,512]{1,0:T(8,128)(2,1)}) fusion(bf16[512,1024]{0,1:T(8,128)(2,1)} %copy-done.1, bf16[512,1024]{0,1:T(8,128)(2,1)} %collective-permute-done.1, pred[]{:T(512)} %bitcast.8, bf16[1024,512]{1,0:T(8,128)(2,1)S(1)} %get-tuple-element.15, ...), kind=kOutput, calls=%fused_computation.18 | convolution fusion | flops 277348352 | bytes 9175556 | tf_op jit(solution)/shard_map/dot_general | solution.py:55
  64.4 10.1 %collective-permute-start.2 = (bf16[512,1024]{0,1:T(8,128)(2,1)}, bf16[512,1024]{0,1:T(8,128)(2,1)S(1)}, u32[]{:S(2)}, u32[]{:S(2)}) collective-permute-start(bf16[512,1024]{0,1:T(8,128)(2,1)} %get-tuple-element.5), channel_id=1, source_target_pairs={{32,0},{48,16},{64,32},{80,48},{96,64},{112,80},{128,96},{144,112}... | collective-permute-start | bytes 3145736 | tf_op jit(solution)/shard_map/ppermute | solution.py:21
  74.6 1.9 collective-permute-start.3
  77.2 2.3 copy.7
  81.0 3.5 %add_convert_fusion.4 = bf16[512,1024]{0,1:T(8,128)(2,1)} fusion(bf16[512,1024]{0,1:T(8,128)(2,1)S(1)} %copy-done.8, bf16[512,512]{1,0:T(8,128)(2,1)} %convolution_convert_fusion.4), kind=kOutput, calls=%fused_computation.13 | convolution fusion | flops 808714240 | bytes 2621440 | tf_op jit(solution)/shard_map/dot_general | solution.py:37
  84.6 3.2 %convolution_convert_fusion.3 = bf16[512,512]{1,0:T(8,128)(2,1)} fusion(bf16[512,1024]{0,1:T(8,128)(2,1)} %add_convert_fusion.4), kind=kOutput, calls=%fused_computation.35 | convolution fusion | flops 537133056 | bytes 1572864 | tf_op jit(solution)/shard_map/dot_general | solution.py:28
  87.7 31.7 %collective-permute-done.2 = bf16[512,1024]{0,1:T(8,128)(2,1)S(1)} collective-permute-done((bf16[512,1024]{0,1:T(8,128)(2,1)}, bf16[512,1024]{0,1:T(8,128)(2,1)S(1)}, u32[]{:S(2)}, u32[]{:S(2)}) %collective-permute-start.2) | collective-permute-done | bytes 1048608 | tf_op jit(solution)/shard_map/ppermute | solution.py:21
  119.5 8.3 %collective-permute-done.3 = bf16[512,1024]{0,1:T(8,128)(2,1)} collective-permute-done((bf16[512,1024]{0,1:T(8,128)(2,1)}, bf16[512,1024]{0,1:T(8,128)(2,1)}, u32[]{:S(2)}, u32[]{:S(2)}) %collective-permute-start.3) | collective-permute-done | bytes 1048608 | tf_op jit(solution)/shard_map/ppermute | solution.py:21
  127.7 2.5 %multiply_reduce_fusion = f32[]{:T(128)} fusion(bf16[1024,512]{1,0:T(8,128)(2,1)S(1)} %copy-done, bf16[512,1024]{0,1:T(8,128)(2,1)S(1)} %get-tuple-element.6, bf16[512,1024]{0,1:T(8,128)(2,1)S(1)} %collective-permute-done.2, bf16[512,1024]{0,1:T(8,128)(2,1)} %collective-permute-done.3, pred[]{:T(512)} %bitcast.15), kind=kLoop, calls=%fused_computation.9 | loop fusion | flops 4718591 | bytes 4194309 | tf_op jit(solution)/shard_map/reduce_sum | solution.py:25
  134.5 2.7 %add_convert_fusion.2 = bf16[512,1024]{0,1:T(8,128)(2,1)S(1)} fusion(bf16[512,1024]{0,1:T(8,128)(2,1)} %copy-done.4, bf16[512,512]{1,0:T(8,128)(2,1)S(1)} %convolution_convert_fusion.1), kind=kOutput, calls=%fused_computation.7 | convolution fusion | flops 808714240 | bytes 2621440 | tf_op jit(solution)/shard_map/dot_general | solution.py:37
  138.0 2.1 add_convert_fusion.1
  140.1 4.7 %fusion.50 = (bf16[512,1024]{0,1:T(8,128)(2,1)}, f32[512,1024]{0,1:T(8,128)S(1)}) fusion(bf16[512,1024]{0,1:T(8,128)(2,1)} %add_convert_fusion.1, bf16[512,1024]{0,1:T(8,128)(2,1)} %add_convert_fusion.4, bf16[512,512]{1,0:T(8,128)(2,1)} %convolution_convert_fusion.3, bf16[1,1,512,1024]{2,3,1,0:T(8,128)(2,1)S(1)} %copy-done.3), kind=kOutput, calls=%fused_computation.87 | convolution fusion | flops 812384256 | bytes 6815744 | tf_op jit(solution)/shard_map/dot_general | solution.py:37
  144.7 1.9 collective-permute-start.4
  146.7 7.3 %collective-permute-start.5 = (bf16[512,1024]{0,1:T(8,128)(2,1)}, bf16[512,1024]{0,1:T(8,128)(2,1)S(1)}, u32[]{:S(2)}, u32[]{:S(2)}) collective-permute-start(bf16[512,1024]{0,1:T(8,128)(2,1)} %get-tuple-element.17), channel_id=1, source_target_pairs={{448,0},{464,16},{480,32},{496,48},{0,64},{16,80},{32,96},{48,112}... | collective-permute-start | bytes 3145736 | tf_op jit(solution)/shard_map/ppermute | solution.py:21
  153.9 86.4 %collective-permute-done.4 = bf16[512,1024]{0,1:T(8,128)(2,1)S(1)} collective-permute-done((bf16[512,1024]{0,1:T(8,128)(2,1)}, bf16[512,1024]{0,1:T(8,128)(2,1)S(1)}, u32[]{:S(2)}, u32[]{:S(2)}) %collective-permute-start.4) | collective-permute-done | bytes 1048608 | tf_op jit(solution)/shard_map/ppermute | solution.py:21
  240.3 3.9 %collective-permute-done.5 = bf16[512,1024]{0,1:T(8,128)(2,1)S(1)} collective-permute-done((bf16[512,1024]{0,1:T(8,128)(2,1)}, bf16[512,1024]{0,1:T(8,128)(2,1)S(1)}, u32[]{:S(2)}, u32[]{:S(2)}) %collective-permute-start.5) | collective-permute-done | bytes 1048608 | tf_op jit(solution)/shard_map/ppermute | solution.py:21
  (37 shorter events, 14.9 us)
Async XLA Ops:
  0.0 10.3 %copy-start.2 = (bf16[1,1,512,1024]{3,2,1,0:T(8,128)(2,1)S(1)}, bf16[1,1,512,1024]{3,2,1,0:T(8,128)(2,1)}, u32[]{:S(2)}) copy-start(bf16[1,1,512,1024]{3,2,1,0:T(8,128)(2,1)} %param.10) | copy-start | bytes 3145732
  1.1 17.5 %copy-start.6 = (bf16[2,1,1,256,512]{4,3,2,1,0:T(8,128)(2,1)S(1)}, bf16[2,1,1,256,512]{4,3,2,1,0:T(8,128)(2,1)}, u32[]{:S(2)}) copy-start(bf16[2,1,1,256,512]{4,3,2,1,0:T(8,128)(2,1)} %param.8) | copy-start | bytes 1572868
  4.2 14.4 %all-to-all-start = ((bf16[16,16,1024]{2,1,0:T(8,128)(2,1)}), bf16[16,16,1024]{2,1,0:T(8,128)(2,1)S(1)}, u32[]{:S(2)}, u32[]{:S(2)}) async-start(bf16[16,16,1024]{2,1,0:T(8,128)(2,1)} %bitcast.4), calls=%async_computation | async-start | bytes 1048576 | tf_op jit(solution)/shard_map/all_to_all | solution.py:80
  18.6 8.4 %copy-start.5 = (bf16[2,1,128,1024]{3,2,1,0:T(8,128)(2,1)S(1)}, bf16[2,1,128,1024]{3,2,1,0:T(8,128)(2,1)}, u32[]{:S(2)}) copy-start(bf16[2,1,128,1024]{3,2,1,0:T(8,128)(2,1)} %param.6) | copy-start | bytes 1572868
  18.6 16.6 %copy-start.7 = (s32[1,2]{1,0:T(1,128)S(1)}, s32[1,2]{1,0:T(1,128)}, u32[]{:S(2)}) copy-start(s32[1,2]{1,0:T(1,128)} %param.11) | copy-start | bytes 28
  20.0 27.5 %collective-permute-start = (bf16[512,1024]{0,1:T(8,128)(2,1)}, bf16[512,1024]{0,1:T(8,128)(2,1)S(1)}, u32[]{:S(2)}, u32[]{:S(2)}) collective-permute-start(bf16[512,1024]{0,1:T(8,128)(2,1)} %get-tuple-element.14), channel_id=1, source_target_pairs={{16,0},{32,16},{48,32},{64,48},{80,64},{96,80},{112,96},{128,112},... | collective-permute-start | bytes 3145736 | tf_op jit(solution)/shard_map/ppermute | solution.py:21
  25.1 33.1 %collective-permute-start.1 = (bf16[512,1024]{0,1:T(8,128)(2,1)}, bf16[512,1024]{0,1:T(8,128)(2,1)}, u32[]{:S(2)}, u32[]{:S(2)}) collective-permute-start(bf16[512,1024]{0,1:T(8,128)(2,1)} %get-tuple-element.14), channel_id=1, source_target_pairs={{496,0},{0,16},{16,32},{32,48},{48,64},{64,80},{80,96},{96,112},{1... | collective-permute-start | bytes 3145736 | tf_op jit(solution)/shard_map/ppermute | solution.py:21
  28.1 32.1 %all-to-all-start.1 = ((bf16[16,16,1024]{2,1,0:T(8,128)(2,1)}), bf16[16,16,1024]{2,1,0:T(8,128)(2,1)}, u32[]{:S(2)}, u32[]{:S(2)}) async-start(bf16[16,16,1024]{2,1,0:T(8,128)(2,1)} %bitcast.11), calls=%async_computation.1 | async-start | bytes 1048576 | tf_op jit(solution)/shard_map/all_to_all | solution.py:80
  47.5 12.0 %copy-start.1 = (bf16[512,1024]{0,1:T(8,128)(2,1)}, bf16[512,1024]{0,1:T(8,128)(2,1)S(1)}, u32[]{:S(2)}) copy-start(bf16[512,1024]{0,1:T(8,128)(2,1)S(1)} %collective-permute-done) | copy-start | bytes 3145732
  64.4 15.0 %copy-start.8 = (bf16[512,1024]{0,1:T(8,128)(2,1)S(1)}, bf16[512,1024]{0,1:T(8,128)(2,1)}, u32[]{:S(2)}) copy-start(bf16[512,1024]{0,1:T(8,128)(2,1)} %get-tuple-element.7) | copy-start | bytes 3145732
  64.4 55.0 %collective-permute-start.2 = (bf16[512,1024]{0,1:T(8,128)(2,1)}, bf16[512,1024]{0,1:T(8,128)(2,1)S(1)}, u32[]{:S(2)}, u32[]{:S(2)}) collective-permute-start(bf16[512,1024]{0,1:T(8,128)(2,1)} %get-tuple-element.5), channel_id=1, source_target_pairs={{32,0},{48,16},{64,32},{80,48},{96,64},{112,80},{128,96},{144,112}... | collective-permute-start | bytes 3145736 | tf_op jit(solution)/shard_map/ppermute | solution.py:21
  74.6 53.2 %collective-permute-start.3 = (bf16[512,1024]{0,1:T(8,128)(2,1)}, bf16[512,1024]{0,1:T(8,128)(2,1)}, u32[]{:S(2)}, u32[]{:S(2)}) collective-permute-start(bf16[512,1024]{0,1:T(8,128)(2,1)} %get-tuple-element.5), channel_id=1, source_target_pairs={{480,0},{496,16},{0,32},{16,48},{32,64},{48,80},{64,96},{80,112},{... | collective-permute-start | bytes 3145736 | tf_op jit(solution)/shard_map/ppermute | solution.py:21
  84.6 43.2 %copy-start = (bf16[1024,512]{1,0:T(8,128)(2,1)S(1)}, bf16[1024,512]{1,0:T(8,128)(2,1)}, u32[]{:S(2)}) copy-start(bf16[1024,512]{1,0:T(8,128)(2,1)} %get-tuple-element.16) | copy-start | bytes 3145732
  132.8 1.0 copy-start.4
  138.0 2.1 copy-start.3
  144.7 95.6 %collective-permute-start.4 = (bf16[512,1024]{0,1:T(8,128)(2,1)}, bf16[512,1024]{0,1:T(8,128)(2,1)S(1)}, u32[]{:S(2)}, u32[]{:S(2)}) collective-permute-start(bf16[512,1024]{0,1:T(8,128)(2,1)} %get-tuple-element.17), channel_id=1, source_target_pairs={{64,0},{80,16},{96,32},{112,48},{128,64},{144,80},{160,96},{176,11... | collective-permute-start | bytes 3145736 | tf_op jit(solution)/shard_map/ppermute | solution.py:21
  146.7 97.5 %collective-permute-start.5 = (bf16[512,1024]{0,1:T(8,128)(2,1)}, bf16[512,1024]{0,1:T(8,128)(2,1)S(1)}, u32[]{:S(2)}, u32[]{:S(2)}) collective-permute-start(bf16[512,1024]{0,1:T(8,128)(2,1)} %get-tuple-element.17), channel_id=1, source_target_pairs={{448,0},{464,16},{480,32},{496,48},{0,64},{16,80},{32,96},{48,112}... | collective-permute-start | bytes 3145736 | tf_op jit(solution)/shard_map/ppermute | solution.py:21

commit v2 on v0

v2 whole, which is shorter than its diff:
```python
import functools
import math

import jax
import jax.numpy as jnp
from jax import lax
from jax.experimental import pallas as pl
from jax.experimental.pallas import tpu as pltpu
from jax.sharding import PartitionSpec as P

MESH = pl.DeviceIdType.MESH
F32 = jnp.float32
BF16 = jnp.bfloat16

coef_a = 3.4445
coef_b = -4.775
coef_c = 2.0315
step_scale = 32.0
HOPS = (1, 2, 4)
CHUNK = 256


def dot_nn(a, b):
    return lax.dot_general(a, b, (((1,), (0,)), ((), ())), preferred_element_type=F32)


def dot_nt(a, b):
    return lax.dot_general(a, b, (((1,), (1,)), ((), ())), preferred_element_type=F32)


def dot_tn(a, b):
    return lax.dot_general(a, b, (((0,), (0,)), ((), ())), preferred_element_type=F32)


def kernel(
    n_sites, n_experts, chunk,
    og_hbm, routes_ref, hid_hbm, w_hbm, off_hbm, bits_ref, out_hbm,
    og, hid, wt, off, placed, arrived, grad, sent, near, tnorm, xmid, moved, out_v,
    gram, gram_b, poly, fro,
    load_sem, a2a_send, a2a_recv, hop_send, hop_recv, out_sem,
):
    site = lax.axis_index("site")
    me = lax.axis_index("expert")
    ff, features = w_hbm.shape
    chunks = features // chunk
    rows = hid.shape[1]
    slots = rows // n_experts
    tokens = og.shape[1]

    def cols(c):
        return pl.ds(pl.multiple_of(c * chunk, chunk), chunk)

    def site_at(distance):
        return lax.rem(site + (distance + n_sites), n_sites)

    def expert_at(d):
        return lax.rem(me + d, n_experts)

    loads = [pltpu.make_async_copy(og_hbm.at[k], og.at[k], load_sem.at[k]) for k in range(2)]
    loads += [pltpu.make_async_copy(hid_hbm.at[k], hid.at[k], load_sem.at[2 + k]) for k in range(2)]

    def off_load(c):
        return pltpu.make_async_copy(off_hbm.at[:, cols(c)], off.at[c], load_sem.at[4 + c])

    def w_load(c):
        return pltpu.make_async_copy(w_hbm.at[:, cols(c)], wt.at[c], load_sem.at[4 + chunks + c])

    loads[0].start()
    loads[2].start()
    for c in range(chunks):
        off_load(c).start()
    loads[1].start()
    loads[3].start()
    for c in range(chunks):
        w_load(c).start()

    barrier = pltpu.get_barrier_semaphore()
    for distance in (1, -1):
        pl.semaphore_signal(barrier, inc=1, device_id={"site": site_at(distance)}, device_id_type=MESH)

    @pl.loop(1, n_experts)
    def _(d):
        pl.semaphore_signal(barrier, inc=1, device_id={"expert": expert_at(d)}, device_id_type=MESH)

    def place(k):
        routing = routes_ref[pl.ds(k, 1), :]
        experts = lax.broadcasted_iota(jnp.int32, (n_experts, tokens), 0)
        owned = jnp.where(experts == routing, 1.0, 0.0)
        early = lax.broadcasted_iota(jnp.int32, (tokens, tokens), 0)
        late = lax.broadcasted_iota(jnp.int32, (tokens, tokens), 1)
        before = jnp.where(early < late, 1.0, 0.0).astype(BF16)
        earlier = dot_nn(owned.astype(BF16), before)
        position = jnp.sum(earlier * owned, axis=0, keepdims=True)
        target = routing.astype(F32) * float(slots) + position
        place_of = lax.broadcasted_iota(jnp.int32, (rows, tokens), 0).astype(F32)
        selector = jnp.where(place_of == target, 1.0, 0.0).astype(BF16)
        placed[k] = dot_nn(selector, og[k]).astype(BF16)
        own = pl.ds(pl.multiple_of(me * slots, slots), slots)
        arrived[k, own, :] = placed[k, own, :]

    def a2a(k, c, d, peer):
        return pltpu.make_async_remote_copy(
            src_ref=placed.at[k, pl.ds(pl.multiple_of(peer * slots, slots), slots), cols(c)],
            dst_ref=arrived.at[k, pl.ds(pl.multiple_of(me * slots, slots), slots), cols(c)],
            send_sem=a2a_send.at[k, c, d - 1],
            recv_sem=a2a_recv.at[k, c, d - 1],
            device_id={"expert": peer},
            device_id_type=MESH,
        )

    def a2a_start(k, c):
        @pl.loop(1, n_experts)
        def _(d):
            a2a(k, c, d, expert_at(d)).start()

    def a2a_wait(k, c):
        @pl.loop(1, n_experts)
        def _(d):
            a2a(k, c, d, expert_at(d)).wait_recv()

    def hop(q, side, c):
        distance = -HOPS[q] if side == 0 else HOPS[q]
        return pltpu.make_async_remote_copy(
            src_ref=sent.at[q, c],
            dst_ref=near.at[q, side, c],
            send_sem=hop_send.at[q, side, c],
            recv_sem=hop_recv.at[q, side, c],
            device_id={"site": site_at(distance)},
            device_id_type=MESH,
        )

    loads[0].wait()
    place(0)
    pl.semaphore_wait(barrier, n_experts + 1)

    @pl.loop(0, chunks)
    def _(c):
        a2a_start(0, c)

    loads[1].wait()
    place(1)
    loads[2].wait()
    loads[3].wait()
    scale = 1.0 / math.sqrt(rows)

    @pl.loop(0, chunks)
    def _(c):
        off_load(c).wait()
        a2a_wait(0, c)
        g = (dot_tn(hid[0], arrived[0, :, cols(c)]) * scale).astype(BF16)
        grad[0, c] = g
        sent[0, c] = (off[c].astype(F32) + g.astype(F32)).astype(BF16)
        hop(0, 0, c).start()
        hop(0, 1, c).start()
        a2a_start(1, c)

    @pl.loop(0, chunks)
    def _(c):
        a2a_wait(1, c)
        grad[1, c] = (dot_tn(hid[1], arrived[1, :, cols(c)]) * scale).astype(BF16)

    def partner(q, c):
        flag = bits_ref[0, q]
        return jnp.where(flag == 1, near[q, 0, c].astype(F32), near[q, 1, c].astype(F32))

    def hop_wait(q, c):
        hop(q, 0, c).wait_recv()
        hop(q, 1, c).wait_recv()

    fro[...] = jnp.zeros_like(fro)

    @pl.loop(0, chunks)
    def _(c):
        hop_wait(0, c)
        g = grad[0, c].astype(F32)
        summed = off[c].astype(F32) + g
        tracked = 0.5 * (summed + partner(0, c))
        second = (tracked - g).astype(BF16).astype(F32) + grad[1, c].astype(F32)
        sent[1, c] = second.astype(BF16)
        hop(1, 0, c).start()
        hop(1, 1, c).start()
        off[c] = (tracked - g).astype(BF16)
        tnorm[c] = tracked.astype(BF16)
        fro[...] += jnp.sum(tracked * tracked, axis=0, keepdims=True)

    def newton_schulz(finish):
        r = 1.0 / (jnp.sqrt(jnp.sum(fro[...], axis=1, keepdims=True)) + 1e-07)
        gram_b[...] = (gram[...] * (r * r)).astype(BF16)

        def polynomial():
            gb = gram_b[...]
            poly[...] = (coef_b * gb.astype(F32) + coef_c * dot_nn(gb, gb)).astype(BF16)

        polynomial()
        gram[...] = jnp.zeros_like(gram)

        @pl.loop(0, chunks)
        def _(c):
            t = tnorm[c]
            x = (r * (coef_a * t.astype(F32) + dot_nn(poly[...], t))).astype(BF16)
            xmid[c] = x
            gram[...] += dot_nt(x, x)

        gram_b[...] = gram[...].astype(BF16)
        polynomial()

        @pl.loop(0, chunks)
        def _(c):
            x = xmid[c]
            finish(c, (coef_a * x.astype(F32) + dot_nn(poly[...], x)).astype(BF16).astype(F32))

    gram[...] = jnp.zeros_like(gram)

    @pl.loop(0, chunks)
    def _(c):
        t = tnorm[c]
        gram[...] += dot_nt(t, t)

    for c in range(chunks):
        w_load(c).wait()

    def finish_first(c, ortho):
        moved[c] = wt[c].astype(F32) - step_scale * ortho

    newton_schulz(finish_first)

    fro[...] = jnp.zeros_like(fro)
    gram[...] = jnp.zeros_like(gram)

    @pl.loop(0, chunks)
    def _(c):
        hop_wait(1, c)
        summed = off[c].astype(F32) + grad[1, c].astype(F32)
        tracked = 0.5 * (summed + partner(1, c))
        fro[...] += jnp.sum(tracked * tracked, axis=0, keepdims=True)
        t = tracked.astype(BF16)
        tnorm[c] = t
        gram[...] += dot_nt(t, t)

    def finish_second(c, ortho):
        m = moved[c] - step_scale * ortho
        sent[2, c] = m.astype(BF16)
        hop(2, 0, c).start()
        hop(2, 1, c).start()
        moved[c] = m

    newton_schulz(finish_second)

    def out_copy(c):
        return pltpu.make_async_copy(out_v.at[c], out_hbm.at[:, cols(c)], out_sem.at[c])

    @pl.loop(0, chunks)
    def _(c):
        hop_wait(2, c)
        beside = near[2, 0, c].astype(F32) + near[2, 1, c].astype(F32)
        out_v[c] = (0.5 * moved[c] + 0.25 * beside).astype(BF16)
        out_copy(c).start()

    @pl.loop(0, chunks)
    def _(c):
        for k in range(2):
            @pl.loop(1, n_experts)
            def _(d):
                a2a(k, c, d, expert_at(d)).wait_send()
        for q in range(3):
            for side in range(2):
                hop(q, side, c).wait_send()
        out_copy(c).wait()


def local(out_grads, routes, hiddens, weights, tracker_offset, partner_bits, chunk=CHUNK):
    n_experts = lax.axis_size("expert")
    n_sites = lax.axis_size("site")
    steps, _, tokens, features = out_grads.shape
    _, _, _, rows, ff = hiddens.shape
    chunks = features // chunk
    block = (chunks, ff, chunk)
    hbm = pl.BlockSpec(memory_space=pl.ANY)
    result = pl.pallas_call(
        functools.partial(kernel, n_sites, n_experts, chunk),
        out_shape=jax.ShapeDtypeStruct((ff, features), BF16),
        in_specs=[
            hbm,
            pl.BlockSpec(memory_space=pltpu.VMEM),
            hbm,
            hbm,
            hbm,
            pl.BlockSpec(memory_space=pltpu.SMEM),
        ],
        out_specs=hbm,
        scratch_shapes=[
            pltpu.VMEM((2, tokens, features), BF16),
            pltpu.VMEM((2, rows, ff), BF16),
            pltpu.VMEM(block, BF16),
            pltpu.VMEM(block, BF16),
            pltpu.VMEM((2, rows, features), BF16),
            pltpu.VMEM((2, rows, features), BF16),
            pltpu.VMEM((2,) + block, BF16),
            pltpu.VMEM((3,) + block, BF16),
            pltpu.VMEM((3, 2) + block, BF16),
            pltpu.VMEM(block, BF16),
            pltpu.VMEM(block, BF16),
            pltpu.VMEM(block, F32),
            pltpu.VMEM(block, BF16),
            pltpu.VMEM((ff, ff), F32),
            pltpu.VMEM((ff, ff), BF16),
            pltpu.VMEM((ff, ff), BF16),
            pltpu.VMEM((1, chunk), F32),
            pltpu.SemaphoreType.DMA((4 + 2 * chunks,)),
            pltpu.SemaphoreType.DMA((2, chunks, n_experts - 1)),
            pltpu.SemaphoreType.DMA((2, chunks, n_experts - 1)),
            pltpu.SemaphoreType.DMA((3, 2, chunks)),
            pltpu.SemaphoreType.DMA((3, 2, chunks)),
            pltpu.SemaphoreType.DMA((chunks,)),
        ],
        compiler_params=pltpu.CompilerParams(collective_id=0, has_side_effects=True),
        name="gossip_muon",
    )(
        out_grads[:, 0],
        routes[:, 0, :, 0],
        hiddens[:, 0, 0],
        weights[0, 0],
        tracker_offset[0, 0],
        partner_bits,
    )
    return result[None, None]


def solution(mesh):
    in_specs = (
        P(None, "site", "expert", None),
        P(None, "site", "expert", None),
        P(None, "site", "expert", None, None),
        P("site", "expert", None, None),
        P("site", "expert", None, None),
        P("site", None),
    )
    out_specs = P("site", "expert", None, None)
    return jax.shard_map(local, mesh=mesh, in_specs=in_specs, out_specs=out_specs, check_vma=False)
```

time: 317 us -> 208 us (0.66)
  the two profiles are of different devices: /device:TPU:104 before, /device:TPU:57 now
where the time goes in v2:
time: 208 us; the launch traced here: 207 us
  Pallas kernels  205 us (99%)
  local copies, waits for them, and re-layouts  2.26 us (1%)
    pallas_call x1, Pallas kernels, local(): pl.pallas_call(functools.partial(kernel, n_sites, n_experts, chunk), out_...  205 us

profile of v2, /device:TPU:57, one launch (start us, length us, event | category | flops | bytes accessed | tf_op | source)
XLA Modules:
  0.0 207.5 jit_solution(13689912327335019183)
XLA Ops:
  0.0 205.2 %gossip_muon.1 = bf16[512,1024]{1,0:T(8,128)(2,1)} custom-call(bf16[2,128,1024]{2,1,0:T(8,128)(2,1)} %bitcast.9, s32[2,128]{1,0:T(2,128)} %bitcast.11, bf16[2,256,512]{2,1,0:T(8,128)(2,1)} %bitcast.10, bf16[512,1024]{1,0:T(8,128)(2,1)} %bitcast.7, bf16[512,1024]{1,0:T(8,128)(2,1)} %bitcast.8, s32[1,2]{1,0:T(1,128)} %bits_ref.1), custom_call_target="tpu_custom_call" | custom-call | tf_op jit(solution)/shard_map/gossip_muon/pallas_call | solution.py:279
  205.2 2.3 %copy.8 = bf16[1,1,512,1024]{3,2,1,0:T(8,128)(2,1)} copy(bf16[1,1,512,1024]{3,2,1,0:T(8,128)(2,1)} %bitcast.6) | data formatting | bytes 2097152
